TPU v7x, 128 devices: a whole 4x4x4 slice. The times are simulated.
128 devices in a mesh: section: 4 (over x), vocab: 2 (over core), dp: 16 (over z, y).
Axes of the slice: x: 4, y: 4, z: 4, core: 2. Of those that a mesh axis runs over, the one named last changes fastest.
Arguments:
- entering: bfloat16 [8, 16, 32, 2048], P(None, 'dp', 'vocab'), may hold values from -6 to 6
- depths: int32 [8], replicated, may hold values from 1 to 4
- targets: int32 [8, 16, 32], P(None, 'dp'), may hold values from 0 to 64127
- norm_gain: float32 [4, 2048], P('section'), may hold values from 0.5 to 1.5
- w_gate: bfloat16 [4, 2048, 7168], P('section', 'dp', 'vocab'), may hold values from -0.125 to 0.125
- w_up: bfloat16 [4, 2048, 7168], P('section', 'dp', 'vocab'), may hold values from -0.125 to 0.125
- w_down: bfloat16 [4, 7168, 2048], P('section', 'vocab', 'dp'), may hold values from -0.0625 to 0.0625
- final_gain: float32 [2048], replicated, may hold values from 0.5 to 1.5
- head_weight: bfloat16 [2048, 64128], P(None, ('section', 'vocab')), may hold values from -32 to 32
Outputs:
- token_loss: float32 [8, 16, 32], P(None, 'dp')
- mean_loss: float32 [], replicated
All inputs are finite; a program needn't handle non-finite values.
Results may differ from a plain program's by a relative error of at most 0.0055.
Values may be sent and summed in bfloat16 or wider, within the bound.
A program may use at most 192 MiB of HBM per device.

v0:
```python
import jax
import jax.numpy as jnp
from jax import lax
from jax.sharding import PartitionSpec as P

EPS = 1e-05


def cut_along(x, dim, size):
    dims = x.shape
    parts = x.reshape(*dims[:dim], size, dims[dim] // size, *dims[dim + 1 :])
    return jnp.moveaxis(parts, dim, 0)


def summed_on_arrival(x, axis, dim):
    size = lax.axis_size(axis)
    parts = lax.all_to_all(cut_along(x, dim, size), axis, 0, 0, tiled=True)
    return jnp.sum(parts, axis=0)


def passed_along(block, axis, distance):
    devices = range(lax.axis_size(axis))
    route = [(i - distance, i) for i in devices if i - distance in devices]
    return lax.ppermute(block, axis, route)


def copy_for_each(x, axis):
    copies = jnp.broadcast_to(x, (lax.axis_size(axis), *x.shape))
    return lax.all_to_all(copies, axis, split_axis=0, concat_axis=0, tiled=True)


def taken_together(x, axis):
    everything = copy_for_each(x, axis)
    return jnp.sum(everything.astype(jnp.float32), axis=0)


def over_copies(x, axis):
    return copy_for_each(x, axis).sum(axis=0)


def rms_scaled(values, gain):
    widened = values.astype(jnp.float32)
    return widened * lax.rsqrt(jnp.mean(widened * widened, axis=-1, keepdims=True) + EPS) * gain


def on_device(entering, depths, targets, norm_gain, w_gate, w_up, w_down, final_gain, head_weight):
    my_segment = lax.axis_index("section")
    micro_count = entering.shape[0]
    row_count = entering.shape[2]
    width = entering.shape[3]
    per_segment = w_gate.shape[0]
    gate_full, up_full, down_full = (
        lax.all_gather(w_gate, "dp", axis=1, tiled=True),
        lax.all_gather(w_up, "dp", axis=1, tiled=True),
        lax.all_gather(w_down, "dp", axis=2, tiled=True),
    )
    local_rows = entering[:, 0]

    def apply_layer(layer_index, current):
        normed = rms_scaled(current, norm_gain[layer_index]).astype(jnp.bfloat16)
        block_rows = lax.all_gather(normed, "vocab", axis=0, tiled=True)
        gate_part = jnp.dot(block_rows, gate_full[layer_index], preferred_element_type=jnp.float32)
        up_part = jnp.dot(block_rows, up_full[layer_index], preferred_element_type=jnp.float32)
        hidden = (jax.nn.silu(gate_part) * up_part).astype(jnp.bfloat16)
        branch = summed_on_arrival(
            jnp.dot(hidden, down_full[layer_index], preferred_element_type=jnp.float32), "vocab", 0
        )
        return (current.astype(jnp.float32) + branch).astype(jnp.bfloat16)

    inject_order = jnp.arange(micro_count, dtype=jnp.int32)

    def advance(step_index, carry):
        current, kept_rows = carry
        slot_index = step_index - my_segment
        is_valid = (slot_index >= 0) & (slot_index < micro_count)
        member = inject_order[jnp.clip(slot_index, 0, micro_count - 1)]
        depth_now = jnp.where(is_valid, depths[member], 0)
        fresh_rows = lax.dynamic_index_in_dim(local_rows, member, 0, keepdims=False)
        current = jnp.where(my_segment == 0, fresh_rows, current)
        updated = apply_layer(0, current)
        current = jnp.where(my_segment * per_segment + 0 < depth_now, updated, current)
        record = is_valid & ((depth_now - 1) // per_segment == my_segment)
        record_value = rms_scaled(current, final_gain).astype(jnp.bfloat16)
        previous = lax.dynamic_index_in_dim(kept_rows, member, 0, keepdims=False)
        kept_rows = lax.dynamic_update_index_in_dim(
            kept_rows, jnp.where(record, record_value, previous), member, 0
        )
        current = passed_along(current, "section", 1)
        return (current, kept_rows)

    start_rows = jnp.zeros((row_count, width), jnp.bfloat16)
    start_kept = jnp.zeros((micro_count, row_count, width), jnp.bfloat16)
    exit_segment = (depths[inject_order] - 1) // per_segment
    step_total = jnp.max(jnp.arange(micro_count, dtype=jnp.int32) + exit_segment) + 1
    current, kept_rows = lax.fori_loop(0, step_total, advance, (start_rows, start_kept))
    finals = (
        taken_together(kept_rows.astype(jnp.float32).astype(jnp.bfloat16), "section")
        .astype(jnp.float32)
        .astype(jnp.bfloat16)
    )
    share_rows = lax.all_gather(finals, "vocab", axis=1, tiled=True)
    labels = targets[:, 0]
    column_count = head_weight.shape[1]
    first_column = (my_segment * lax.axis_size("vocab") + lax.axis_index("vocab")) * column_count
    logits = jnp.einsum("mpd,dc->mpc", share_rows, head_weight, preferred_element_type=jnp.float32)
    columns = first_column + jnp.arange(column_count, dtype=jnp.int32)
    picked = jnp.sum(jnp.where(columns == labels[:, :, None], logits, 0.0), axis=-1)
    local_peak = jnp.max(logits, axis=-1)
    peak_all = lax.pmax(local_peak, ("section", "vocab"))
    local_total = jnp.sum(jnp.exp(logits - peak_all[:, :, None]), axis=-1)
    totals, target_logit = lax.psum((local_total, picked), ("section", "vocab"))
    losses = jnp.log(totals) + peak_all - target_logit
    share_sum = over_copies(jnp.sum(losses), "dp")
    mean_loss = share_sum / float(micro_count * lax.axis_size("dp") * losses.shape[1])
    return (losses[:, None, :], mean_loss)


def solution(mesh):
    in_specs = (
        P(None, "dp", "vocab", None),
        P(),
        P(None, "dp", None),
        P("section", None),
        P("section", "dp", "vocab"),
        P("section", "dp", "vocab"),
        P("section", "vocab", "dp"),
        P(),
        P(None, ("section", "vocab")),
    )
    out_specs = (P(None, "dp", None), P())
    return jax.shard_map(
        on_device, mesh=mesh, in_specs=in_specs, out_specs=out_specs, check_vma=False
    )
```

profile of v0, /device:TPU:1, one launch (start us, length us, event | category | flops | bytes accessed | tf_op | source)
XLA Modules:
  0.0 764.4 jit_solution(16884328815172958078)
XLA Ops:
  12.1 101.7 %all-gather.5.cloned.1.call-done = bf16[1,2048,3584]{2,1,0:T(8,128)(2,1)} async-done(((bf16[1,128,3584]{2,1,0:T(8,128)(2,1)}), bf16[1,2048,3584]{2,1,0:T(8,128)(2,1)}) %all-gather.5.cloned.1.call-update) | async-done | bytes 14680080 | tf_op jit(solution)/shard_map/all_gather | solution.py:53
  113.8 102.4 %all-gather.7.cloned.1.call-done = bf16[1,2048,3584]{2,1,0:T(8,128)(2,1)} async-done(((bf16[1,128,3584]{2,1,0:T(8,128)(2,1)}), bf16[1,2048,3584]{2,1,0:T(8,128)(2,1)}) %all-gather.7.cloned.1.call-update) | async-done | bytes 14680080 | tf_op jit(solution)/shard_map/all_gather | solution.py:54
  216.2 109.8 %all-gather.9.cloned.1.call-done = bf16[1,3584,2048]{2,1,0:T(8,128)(2,1)} async-done(((bf16[1,3584,128]{2,1,0:T(8,128)(2,1)}), bf16[1,3584,2048]{2,1,0:T(8,128)(2,1)}) %all-gather.9.cloned.1.call-update) | async-done | bytes 14680080 | tf_op jit(solution)/shard_map/all_gather | solution.py:55
  326.1 322.0 %while.15 = (s32[]{:T(128)}, bf16[16,2048]{1,0:T(8,128)(2,1)S(1)}, bf16[8,16,2048]{2,1,0:T(8,128)(2,1)S(1)}, s32[]{:T(128)}, s32[]{:T(128)}, /*index=5*/s32[8]{0...) while((s32[]{:T(128)}, bf16[16,2048]{1,0:T(8,128)(2,1)S(1)}, ...), condition=%wide.region_5.6_spmd, body=%wide.region_1.5_spmd.sunk | while | flops 1410662400 | bytes 151307984 | solution.py:95
  334.6 7.9 %fusion.53 = f32[32,3584]{1,0:T(8,128)S(1)} fusion(bf16[32,2048]{1,0:T(8,128)(2,1)S(1)} %all_gather.24, bf16[1,2048,3584]{2,1,0:T(8,128)(2,1)} %get-tuple-element.398), kind=kOutput, calls=%fused_computation.5.clone.1 | convolution fusion | flops 469762048 | bytes 15269888 | tf_op jit(solution)/shard_map/while/body/dot_general | solution.py:62
  365.9 7.9 %fusion.53 = f32[32,3584]{1,0:T(8,128)S(1)} fusion(bf16[32,2048]{1,0:T(8,128)(2,1)S(1)} %all_gather.24, bf16[1,2048,3584]{2,1,0:T(8,128)(2,1)} %get-tuple-element.398), kind=kOutput, calls=%fused_computation.5.clone.1 | convolution fusion | flops 469762048 | bytes 15269888 | tf_op jit(solution)/shard_map/while/body/dot_general | solution.py:62
  380.0 3.8 all-to-all-start
  385.1 4.0 collective-permute-start
  398.1 7.9 %fusion.53 = f32[32,3584]{1,0:T(8,128)S(1)} fusion(bf16[32,2048]{1,0:T(8,128)(2,1)S(1)} %all_gather.24, bf16[1,2048,3584]{2,1,0:T(8,128)(2,1)} %get-tuple-element.398), kind=kOutput, calls=%fused_computation.5.clone.1 | convolution fusion | flops 469762048 | bytes 15269888 | tf_op jit(solution)/shard_map/while/body/dot_general | solution.py:62
  417.3 4.0 collective-permute-start
  430.3 7.9 %fusion.53 = f32[32,3584]{1,0:T(8,128)S(1)} fusion(bf16[32,2048]{1,0:T(8,128)(2,1)S(1)} %all_gather.24, bf16[1,2048,3584]{2,1,0:T(8,128)(2,1)} %get-tuple-element.398), kind=kOutput, calls=%fused_computation.5.clone.1 | convolution fusion | flops 469762048 | bytes 15269888 | tf_op jit(solution)/shard_map/while/body/dot_general | solution.py:62
  444.4 3.8 all-to-all-start
  449.6 4.0 collective-permute-start
  462.5 7.9 %fusion.53 = f32[32,3584]{1,0:T(8,128)S(1)} fusion(bf16[32,2048]{1,0:T(8,128)(2,1)S(1)} %all_gather.24, bf16[1,2048,3584]{2,1,0:T(8,128)(2,1)} %get-tuple-element.398), kind=kOutput, calls=%fused_computation.5.clone.1 | convolution fusion | flops 469762048 | bytes 15269888 | tf_op jit(solution)/shard_map/while/body/dot_general | solution.py:62
  481.8 4.0 collective-permute-start
  494.7 7.9 %fusion.53 = f32[32,3584]{1,0:T(8,128)S(1)} fusion(bf16[32,2048]{1,0:T(8,128)(2,1)S(1)} %all_gather.24, bf16[1,2048,3584]{2,1,0:T(8,128)(2,1)} %get-tuple-element.398), kind=kOutput, calls=%fused_computation.5.clone.1 | convolution fusion | flops 469762048 | bytes 15269888 | tf_op jit(solution)/shard_map/while/body/dot_general | solution.py:62
  514.0 4.0 collective-permute-start
  526.9 7.9 %fusion.53 = f32[32,3584]{1,0:T(8,128)S(1)} fusion(bf16[32,2048]{1,0:T(8,128)(2,1)S(1)} %all_gather.24, bf16[1,2048,3584]{2,1,0:T(8,128)(2,1)} %get-tuple-element.398), kind=kOutput, calls=%fused_computation.5.clone.1 | convolution fusion | flops 469762048 | bytes 15269888 | tf_op jit(solution)/shard_map/while/body/dot_general | solution.py:62
  546.2 4.0 collective-permute-start
  559.1 7.9 %fusion.53 = f32[32,3584]{1,0:T(8,128)S(1)} fusion(bf16[32,2048]{1,0:T(8,128)(2,1)S(1)} %all_gather.24, bf16[1,2048,3584]{2,1,0:T(8,128)(2,1)} %get-tuple-element.398), kind=kOutput, calls=%fused_computation.5.clone.1 | convolution fusion | flops 469762048 | bytes 15269888 | tf_op jit(solution)/shard_map/while/body/dot_general | solution.py:62
  578.4 4.0 collective-permute-start
  591.3 7.9 %fusion.53 = f32[32,3584]{1,0:T(8,128)S(1)} fusion(bf16[32,2048]{1,0:T(8,128)(2,1)S(1)} %all_gather.24, bf16[1,2048,3584]{2,1,0:T(8,128)(2,1)} %get-tuple-element.398), kind=kOutput, calls=%fused_computation.5.clone.1 | convolution fusion | flops 469762048 | bytes 15269888 | tf_op jit(solution)/shard_map/while/body/dot_general | solution.py:62
  610.6 4.0 collective-permute-start
  623.5 7.9 %fusion.53 = f32[32,3584]{1,0:T(8,128)S(1)} fusion(bf16[32,2048]{1,0:T(8,128)(2,1)S(1)} %all_gather.24, bf16[1,2048,3584]{2,1,0:T(8,128)(2,1)} %get-tuple-element.398), kind=kOutput, calls=%fused_computation.5.clone.1 | convolution fusion | flops 469762048 | bytes 15269888 | tf_op jit(solution)/shard_map/while/body/dot_general | solution.py:62
  642.8 4.0 collective-permute-start
  648.3 29.0 %all_to_all.21 = bf16[4,8,16,2048]{3,2,1,0:T(8,128)(2,1)S(1)} all-to-all(bf16[4,8,16,2048]{3,2,1,0:T(8,128)(2,1)S(1)} %broadcast_in_dim.35), channel_id=1, replica_groups=mesh['section'=4,'vocab'=2,'dp'=16] {'section'}, dimensions={0} | all-to-all | bytes 4194304 | tf_op jit(solution)/shard_map/all_to_all | solution.py:29
  678.7 11.7 %all-gather.11.cloned.1.call-done = bf16[8,32,2048]{2,1,0:T(8,128)(2,1)} async-done(((bf16[8,16,2048]{2,1,0:T(8,128)(2,1)}), bf16[8,32,2048]{2,1,0:T(8,128)(2,1)}) %all-gather.11.cloned.1.call-update) | async-done | bytes 1048592 | tf_op jit(solution)/shard_map/all_gather | solution.py:101
  690.4 18.4 %fusion.27 = (f32[8,32]{1,0:T(8,128)S(1)}, f32[8,32,8016]{2,1,0:T(8,128)}) fusion(bf16[8,32,2048]{2,1,0:T(8,128)(2,1)} %all-gather.11.cloned.1.call-done, bf16[2048,8016]{0,1:T(8,128)(2,1)} %param.19), kind=kOutput, calls=%fused_computation.38 | convolution fusion | flops 8407437312 | bytes 42091520 | tf_op jit(solution)/shard_map/mpd,dc->mpc/dot_general | solution.py:105
  708.8 12.0 %pmax.7 = f32[8,32]{1,0:T(8,128)S(1)} all-reduce(f32[8,32]{1,0:T(8,128)S(1)} %get-tuple-element.252), channel_id=1, replica_groups=mesh['section'=4,'vocab'=2,'dp'=16] {'section','vocab'}, use_global_device_ids=true, to_apply=%region_8.9 | all-reduce | flops 256 | bytes 2048 | tf_op jit(solution)/shard_map/pmax | solution.py:109
  720.8 4.6 exponential_reduce_fusion
  725.4 15.3 %all-reduce = (f32[8,32]{1,0:T(8,128)S(1)}, f32[8,32]{1,0:T(8,128)S(1)}) all-reduce(f32[8,32]{1,0:T(8,128)S(1)} %get-tuple-element.215, f32[8,32]{1,0:T(8,128)S(1)} %get-tuple-element.214), channel_id=1, replica_groups=mesh['section'=4,'vocab'=2,'dp'=16] {'section','vocab'}, use_global_device_ids=true, to_apply=%region_12.13 | all-reduce | flops 512 | bytes 4096 | tf_op jit(solution)/shard_map/psum | solution.py:111
  742.5 12.9 %all_to_all.22 = f32[16,1,1]{2,1,0:T(1,128)S(1)} all-to-all(f32[16,1,1]{2,1,0:T(1,128)S(1)} %broadcast_in_dim.38), channel_id=1, replica_groups=mesh['section'=4,'vocab'=2,'dp'=16] {'dp'}, dimensions={0} | all-to-all | bytes 128 | tf_op jit(solution)/shard_map/all_to_all | solution.py:29
  (332 shorter events, 181.8 us)
Async XLA Ops:
  7.2 106.6 %all-gather.5.cloned.1.call-start = ((), (), s32[]{:S(2)}) async-start(), calls=%async_computation.3 | async-start | bytes 15597568 | tf_op jit(solution)/shard_map/all_gather | solution.py:53
  7.9 208.3 %all-gather.7.cloned.1.call-start = ((), (), s32[]{:S(2)}) async-start(), calls=%async_computation.4 | async-start | bytes 15597568 | tf_op jit(solution)/shard_map/all_gather | solution.py:54
  8.6 317.4 %all-gather.9.cloned.1.call-start = ((), (), s32[]{:S(2)}) async-start(), calls=%async_computation.5 | async-start | bytes 15597568 | tf_op jit(solution)/shard_map/all_gather | solution.py:55
  9.4 681.0 %all-gather.11.cloned.1.call-start = ((), (), s32[]{:S(2)}) async-start(), calls=%async_computation.6 | async-start | bytes 1572864 | tf_op jit(solution)/shard_map/all_gather | solution.py:101
  348.7 5.0 all-to-all-start
  353.8 4.4 collective-permute-start
  380.0 5.0 all-to-all-start
  385.1 5.3 collective-permute-start
  406.0 15.4 %copy-start.2 = (f32[2048]{0:T(1024)S(1)}, f32[2048]{0:T(1024)}, u32[]{:S(2)}) copy-start(f32[2048]{0:T(1024)} %get-tuple-element.401) | copy-start | bytes 24580 | tf_op jit(solution)/shard_map/while
  412.2 5.0 all-to-all-start
  417.3 5.3 collective-permute-start
  438.2 15.4 %copy-start.2 = (f32[2048]{0:T(1024)S(1)}, f32[2048]{0:T(1024)}, u32[]{:S(2)}) copy-start(f32[2048]{0:T(1024)} %get-tuple-element.401) | copy-start | bytes 24580 | tf_op jit(solution)/shard_map/while
  444.4 5.0 all-to-all-start
  449.6 5.3 collective-permute-start
  470.4 15.4 %copy-start.2 = (f32[2048]{0:T(1024)S(1)}, f32[2048]{0:T(1024)}, u32[]{:S(2)}) copy-start(f32[2048]{0:T(1024)} %get-tuple-element.401) | copy-start | bytes 24580 | tf_op jit(solution)/shard_map/while
  476.6 5.0 all-to-all-start
  481.8 5.3 collective-permute-start
  508.8 5.0 all-to-all-start
  514.0 5.3 collective-permute-start
  534.8 15.4 %copy-start.2 = (f32[2048]{0:T(1024)S(1)}, f32[2048]{0:T(1024)}, u32[]{:S(2)}) copy-start(f32[2048]{0:T(1024)} %get-tuple-element.401) | copy-start | bytes 24580 | tf_op jit(solution)/shard_map/while
  541.0 5.0 all-to-all-start
  546.2 5.3 collective-permute-start
  567.1 15.4 %copy-start.2 = (f32[2048]{0:T(1024)S(1)}, f32[2048]{0:T(1024)}, u32[]{:S(2)}) copy-start(f32[2048]{0:T(1024)} %get-tuple-element.401) | copy-start | bytes 24580 | tf_op jit(solution)/shard_map/while
  573.2 5.0 all-to-all-start
  578.4 5.3 collective-permute-start
  599.3 15.4 %copy-start.2 = (f32[2048]{0:T(1024)S(1)}, f32[2048]{0:T(1024)}, u32[]{:S(2)}) copy-start(f32[2048]{0:T(1024)} %get-tuple-element.401) | copy-start | bytes 24580 | tf_op jit(solution)/shard_map/while
  605.4 5.0 all-to-all-start
  610.6 5.3 collective-permute-start
  631.5 15.4 %copy-start.2 = (f32[2048]{0:T(1024)S(1)}, f32[2048]{0:T(1024)}, u32[]{:S(2)}) copy-start(f32[2048]{0:T(1024)} %get-tuple-element.401) | copy-start | bytes 24580 | tf_op jit(solution)/shard_map/while
  637.6 5.0 all-to-all-start
  642.8 5.3 collective-permute-start
  678.7 42.1 %copy-start.3 = (s32[8,1,32]{2,1,0:T(1,128)S(1)}, s32[8,1,32]{2,1,0:T(1,128)}, u32[]{:S(2)}) copy-start(s32[8,1,32]{2,1,0:T(1,128)} %param.13) | copy-start | bytes 3076
  (63 other events, 541.6 us)
Sparse Core Ops, SparseCore 0:
  10.1 103.6 all-gather.4
  115.9 100.1 all-gather.6
  218.3 107.6 all-gather.8
  678.8 11.5 all-gather.10
where the time goes:
time: 751 us; the launch traced here: 764 us
  waiting for transfers between devices  340 us (45%)
  matrix products  156 us (21%)
  blocking collectives  98.9 us (13%)
  starting transfers between devices  76.9 us (10%)
  other arithmetic  32.8 us (4%)
  loops' own time  26.3 us (4%)
  local copies, waits for them, and re-layouts  17.2 us (2%)
  between operations  16.3 us (2%)
    all_gather x1, waiting for transfers between devices, on_device(): lax.all_gather(w_down, 'dp', axis=2, tiled=True)  110 us
    all_gather x1, waiting for transfers between devices, on_device(): lax.all_gather(w_up, 'dp', axis=1, tiled=True)  102 us
    all_gather x1, waiting for transfers between devices, on_device(): lax.all_gather(w_gate, 'dp', axis=1, tiled=True)  102 us
    dot_general x10, matrix products, apply_layer(): jnp.dot(block_rows, gate_full[layer_index], preferred_element_type=jnp.fl...  78.8 us
    all_to_all x2, blocking collectives, copy_for_each(): return lax.all_to_all(copies, axis, split_axis=0, concat_axis=0, tiled=True)  41.9 us
    ppermute x10, starting transfers between devices, passed_along(): return lax.ppermute(block, axis, route)  38.9 us
    all_to_all x10, starting transfers between devices, summed_on_arrival(): parts = lax.all_to_all(cut_along(x, dim, size), axis, 0, 0, tiled=True)  37.9 us
    dot_general x10, matrix products, apply_layer(): jnp.dot(hidden, down_full[layer_index], preferred_element_type=jnp.float32)  33.3 us
  transfers between devices with their start and end apart: 24, of which 14 were waited for; matrix products, arithmetic and copies ran while one was open for 1% of the time, Pallas kernels for 0%

commit v1 on v0

v1 whole, which is shorter than its diff:
```python
import functools

import jax
import jax.numpy as jnp
from jax import lax
from jax.experimental import pallas as pl
from jax.experimental.pallas import tpu as pltpu
from jax.sharding import PartitionSpec as P

EPS = 1e-05
MESH = pl.DeviceIdType.MESH
SIDE = 4


def rms_scaled(values, gain):
    widened = values.astype(jnp.float32)
    return widened * lax.rsqrt(jnp.mean(widened * widened, axis=-1, keepdims=True) + EPS) * gain


def place():
    s, v, i = lax.axis_index("section"), lax.axis_index("vocab"), lax.axis_index("dp")
    z, y = lax.div(i, SIDE), lax.rem(i, SIDE)
    return s, v, i, y + v * (z - y), z + v * (y - z)


def dp_of(v, a, b):
    return SIDE * b + a + v * (SIDE - 1) * (a - b)


def turned(x, d):
    return lax.rem(x + d, SIDE)


def layers_kernel(
    ent_ref, act_ref, gain_ref, fgain_ref, wg_ref, wu_ref, wd_ref, fin_ref,
    wgu, wdn, gat, part, arr, xin, xout, hid,
    own_sem, w_send, w_recv, ag_send, ag_recv, rs_send, rs_recv, x_send, x_recv, f_send, f_recv,
):
    s, v, i, a, b = place()
    micro, half, width = ent_ref.shape
    hb = hid.shape[1]
    fr = wg_ref.shape[0]
    w_other = 1 - v
    last = SIDE - 1

    def to(src, dst, send, recv, where):
        return pltpu.make_async_remote_copy(
            src_ref=src, dst_ref=dst, send_sem=send, recv_sem=recv, device_id=where, device_id_type=MESH
        )

    barrier = pltpu.get_barrier_semaphore()
    for w in (0, 1):
        for d in range(1, SIDE):
            pl.semaphore_signal(barrier, inc=1, device_id=(s, w, dp_of(v, turned(a, d), b)), device_id_type=MESH)
            pl.semaphore_signal(barrier, inc=1, device_id=(s, w, dp_of(v, a, turned(b, d))), device_id_type=MESH)
            pl.semaphore_signal(barrier, inc=1, device_id=(turned(s, d), w, i), device_id_type=MESH)
    pl.semaphore_signal(barrier, inc=1, device_id=(s, w_other, i), device_id_type=MESH)
    pl.semaphore_wait(barrier, 6 * last + 1)

    def landing(k):
        rows = pl.ds(pl.multiple_of(k * fr, fr), fr)
        return wgu.at[rows, pl.ds(0, hb)], wgu.at[rows, pl.ds(hb, hb)], wdn.at[:, rows]

    def held(k):
        units = pl.ds(pl.multiple_of(k * hb, hb), hb)
        return wg_ref.at[:, units], wu_ref.at[:, units], wd_ref.at[units, :]

    def three(sources, k, send, recv, where):
        for src, dst in zip(sources, landing(k)):
            to(src, dst, send, recv, where).start()

    three_bytes = wgu.at[pl.ds(0, 3 * fr), pl.ds(0, hb)]

    def await_block(j, d):
        sem = w_recv.at[turned(a, j) * SIDE + turned(b, d)]
        pltpu.make_async_copy(three_bytes, three_bytes, sem).wait()

    right = (s, v, dp_of(v, a, turned(b, 1)))
    left = (s, v, dp_of(v, a, turned(b, last)))

    def pass_round(j, sources):
        k = dp_of(v, turned(a, j), b)
        recv = w_recv.at[turned(a, j) * SIDE + b]
        three(sources, k, w_send.at[3 + 2 * j], recv, right)
        three(sources, k, w_send.at[4 + 2 * j], recv, left)

    for src, dst in zip(held(a), landing(i)):
        pltpu.make_async_copy(src, dst, own_sem).start()
    for d in range(1, SIDE):
        peer = turned(a, d)
        three(held(peer), i, w_send.at[d - 1], w_recv.at[a * SIDE + b], (s, v, dp_of(v, peer, b)))
    pass_round(0, held(a))

    def to_group(src, block_own, block_other, send, recv):
        for d in range(1, SIDE):
            to(src, gat.at[block_own], send, recv, (s, v, dp_of(v, turned(a, d), b))).start()
        for d in range(SIDE):
            to(src, gat.at[block_other], send, recv, (s, w_other, dp_of(v, a, turned(b, d)))).start()

    def enter(m):
        @pl.when(s == 0)
        def _():
            xin[m] = ent_ref[m]

        @pl.when(s > 0)
        def _():
            pltpu.make_async_copy(xin.at[m], xin.at[m], x_recv.at[m]).wait()

        mine = m * 8 + a * 2 + v
        gat[mine] = rms_scaled(xin[m], gain_ref[...]).astype(jnp.bfloat16)
        to_group(gat.at[mine], mine, m * 8 + b * 2 + v, ag_send.at[m], ag_recv.at[m])

    def branch(m):
        seven = gat.at[pl.ds(0, 7)]
        pltpu.make_async_copy(seven, seven, ag_recv.at[m]).wait()
        rows = gat[pl.ds(pl.multiple_of(m * 8, 8), 8)].reshape(8 * half, width)
        both = jnp.dot(rows, wgu[...], preferred_element_type=jnp.float32)
        gate, up = both[:, :hb], both[:, hb:]
        hid[...] = (gate / (1.0 + jnp.exp(-gate)) * up).astype(jnp.bfloat16)
        out = jnp.dot(hid[...], wdn[...], preferred_element_type=jnp.float32)
        part[pl.ds(pl.multiple_of(m * 8, 8), 8)] = out.astype(jnp.bfloat16).reshape(8, half, width)
        slot = m * 8 + v * SIDE + a
        for d in range(1, SIDE):
            c = turned(a, d)
            for w in (0, 1):
                to(part.at[m * 8 + c * 2 + w], arr.at[slot], rs_send.at[m], rs_recv.at[m],
                   (s, w, dp_of(v, c, b))).start()
        to(part.at[m * 8 + a * 2 + w_other], arr.at[slot], rs_send.at[m], rs_recv.at[m], (s, w_other, i)).start()
        arr[slot] = part[m * 8 + a * 2 + v]

    def leave(m):
        seven = arr.at[pl.ds(0, 7)]
        pltpu.make_async_copy(seven, seven, rs_recv.at[m]).wait()
        total = arr[m * 8].astype(jnp.float32)
        for k in range(1, 8):
            total = total + arr[m * 8 + k].astype(jnp.float32)
        state = xin[m].astype(jnp.float32)
        state = jnp.where(act_ref[m] > 0.0, state + total, state).astype(jnp.bfloat16)

        @pl.when(s < last)
        def _():
            xout[m] = state
            to(xout.at[m], xin.at[m], x_send.at[m], x_recv.at[m], (s + 1, v, i)).start()

        @pl.when(s == last)
        def _():
            fin_ref[m * 2 + v] = rms_scaled(state, fgain_ref[...]).astype(jnp.bfloat16)
            mine = fin_ref.at[m * 2 + v]
            for d in range(1, SIDE):
                for w in (0, 1):
                    to(mine, mine, f_send.at[m], f_recv, (turned(s, d), w, i)).start()
            to(mine, mine, f_send.at[m], f_recv, (s, w_other, i)).start()

    enter(0)
    enter(1)

    for j in range(1, SIDE):
        await_block(j, 0)
        pass_round(j, landing(dp_of(v, turned(a, j), b)))
    for j in range(SIDE):
        d, where = (last, right) if j % 2 == 0 else (1, left)
        await_block(j, d)
        k = dp_of(v, turned(a, j), turned(b, d))
        three(landing(k), k, w_send.at[11 + j], w_recv.at[turned(a, j) * SIDE + turned(b, d)], where)
        await_block(j, SIDE - d)
    for j in range(SIDE):
        await_block(j, 2)
    pltpu.make_async_copy(three_bytes, three_bytes, own_sem).wait()

    def step(m, carry):
        branch(m)

        @pl.when(m > 0)
        def _():
            leave(m - 1)

        @pl.when(m + 2 < micro)
        def _():
            enter(m + 2)

        return carry

    lax.fori_loop(0, micro, step, 0)
    leave(micro - 1)

    @pl.when(s < last)
    def _():
        pltpu.make_async_copy(fin_ref, fin_ref, f_recv).wait()

    @pl.when(s == last)
    def _():
        others = fin_ref.at[pl.ds(0, micro)]
        pltpu.make_async_copy(others, others, f_recv).wait()

    for k in range(15):
        pltpu.make_async_copy(three_bytes, three_bytes, w_send.at[k]).wait()

    def drain(m, carry):
        seven, one = gat.at[pl.ds(0, 7)], xout.at[0]
        pltpu.make_async_copy(seven, seven, ag_send.at[m]).wait()
        pltpu.make_async_copy(seven, seven, rs_send.at[m]).wait()

        @pl.when(s < last)
        def _():
            pltpu.make_async_copy(one, one, x_send.at[m]).wait()

        @pl.when(s == last)
        def _():
            pltpu.make_async_copy(seven, seven, f_send.at[m]).wait()

        return carry

    lax.fori_loop(0, micro, drain, 0)


def through_layers(rows, active, gain, final_gain, w_gate, w_up, w_down):
    micro, half, width = rows.shape
    hb = w_gate.shape[1] // SIDE
    vmem, any_space = pl.BlockSpec(memory_space=pltpu.VMEM), pl.BlockSpec(memory_space=pl.ANY)
    dma = pltpu.SemaphoreType.DMA
    bf16 = jnp.bfloat16
    return pl.pallas_call(
        layers_kernel,
        out_shape=jax.ShapeDtypeStruct((2 * micro, half, width), bf16),
        in_specs=[vmem] * 4 + [any_space] * 3,
        out_specs=vmem,
        scratch_shapes=[
            pltpu.VMEM((width, 2 * hb), bf16),
            pltpu.VMEM((hb, width), bf16),
            pltpu.VMEM((micro * 8, half, width), bf16),
            pltpu.VMEM((micro * 8, half, width), bf16),
            pltpu.VMEM((micro * 8, half, width), bf16),
            pltpu.VMEM((micro, half, width), bf16),
            pltpu.VMEM((micro, half, width), bf16),
            pltpu.VMEM((8 * half, hb), bf16),
            dma(()), dma((15,)), dma((SIDE * SIDE,)),
            dma((micro,)), dma((micro,)), dma((micro,)), dma((micro,)),
            dma((micro,)), dma((micro,)), dma((micro,)), dma(()),
        ],
        compiler_params=pltpu.CompilerParams(
            collective_id=0, has_side_effects=True, vmem_limit_bytes=56 * 1024 * 1024
        ),
        name="layers",
    )(rows, active, gain, final_gain, w_gate, w_up, w_down)


def head_kernel(columns, fin_ref, head_ref, label_ref, out_ref, peak, total, picked):
    j = pl.program_id(0)
    rows, lanes = peak.shape
    tile = head_ref.shape[1]

    @pl.when(j == 0)
    def _():
        peak[...] = jnp.full_like(peak, -1e30)
        total[...] = jnp.zeros_like(total)
        picked[...] = jnp.zeros_like(picked)

    logits = jnp.dot(fin_ref[...], head_ref[...], preferred_element_type=jnp.float32)
    at = j * tile + lax.broadcasted_iota(jnp.int32, (rows, lanes), 1)
    groups = []
    for g in range(tile // lanes):
        groups.append(jnp.where(at + g * lanes < columns, logits[:, g * lanes : (g + 1) * lanes], -1e30))
    old = peak[...]
    new = old
    for values in groups:
        new = jnp.maximum(new, values)
    summed = total[...] * jnp.exp(old - new)
    found = picked[...]
    label = label_ref[...]
    for g, values in enumerate(groups):
        summed = summed + jnp.exp(values - new)
        found = found + jnp.where(at + g * lanes == label, values, 0.0)
    peak[...], total[...], picked[...] = new, summed, found

    @pl.when(j == pl.num_programs(0) - 1)
    def _():
        top = jnp.max(new, axis=1, keepdims=True)
        whole = jnp.sum(summed * jnp.exp(new - top), axis=1, keepdims=True)
        mine = jnp.sum(found, axis=1, keepdims=True)
        for k, column in enumerate((top, whole, mine)):
            out_ref[k : k + 1, :] = jnp.transpose(jnp.broadcast_to(column, (rows, lanes)))[0:1, :]
        out_ref[3:8, :] = jnp.zeros((5, rows), jnp.float32)


def head_sums(finals, head_weight, labels, tile=1024):
    rows, width = finals.shape
    columns = head_weight.shape[1]
    return pl.pallas_call(
        functools.partial(head_kernel, columns),
        out_shape=jax.ShapeDtypeStruct((8, rows), jnp.float32),
        grid=(pl.cdiv(columns, tile),),
        in_specs=[
            pl.BlockSpec((rows, width), lambda j: (0, 0)),
            pl.BlockSpec((width, tile), lambda j: (0, j)),
            pl.BlockSpec((rows, 128), lambda j: (0, 0)),
        ],
        out_specs=pl.BlockSpec((8, rows), lambda j: (0, 0)),
        scratch_shapes=[pltpu.VMEM((rows, 128), jnp.float32)] * 3,
        compiler_params=pltpu.CompilerParams(vmem_limit_bytes=40 * 1024 * 1024),
        name="head",
    )(finals, head_weight, labels)


def losses_kernel(count, sums_ref, loss_ref, mean_ref, shared, totals, own, s_send, s_recv, t_send, t_recv):
    s, v, i = lax.axis_index("section"), lax.axis_index("vocab"), lax.axis_index("dp")
    shards, shares = 8, totals.shape[0]
    barrier = pltpu.get_barrier_semaphore()
    me = s * 2 + v
    for d in range(1, shards):
        k = lax.rem(me + d, shards)
        pl.semaphore_signal(
            barrier, inc=1, device_id=(lax.div(k, 2), lax.rem(k, 2), i), device_id_type=MESH
        )
    for d in range(1, shares):
        pl.semaphore_signal(barrier, inc=1, device_id=(s, v, lax.rem(i + d, shares)), device_id_type=MESH)
    pl.semaphore_wait(barrier, shards + shares - 2)

    for d in range(1, shards):
        k = lax.rem(me + d, shards)
        pltpu.make_async_remote_copy(
            src_ref=sums_ref, dst_ref=shared.at[me], send_sem=s_send, recv_sem=s_recv,
            device_id=(lax.div(k, 2), lax.rem(k, 2), i), device_id_type=MESH,
        ).start()
    shared[me] = sums_ref[...]
    seven = shared.at[pl.ds(0, shards - 1)]
    pltpu.make_async_copy(seven, seven, s_recv).wait()
    everyone = shared[...]
    peaks = everyone[:, 0, :]
    peak = jnp.max(peaks, axis=0, keepdims=True)
    total = jnp.sum(everyone[:, 1, :] * jnp.exp(peaks - peak), axis=0, keepdims=True)
    picked = jnp.sum(everyone[:, 2, :], axis=0, keepdims=True)
    loss = jnp.log(total) + peak - picked
    loss_ref[...] = loss
    own[...] = jnp.broadcast_to(jnp.sum(loss, axis=1, keepdims=True), own.shape)
    for d in range(1, shares):
        pltpu.make_async_remote_copy(
            src_ref=own, dst_ref=totals.at[i], send_sem=t_send, recv_sem=t_recv,
            device_id=(s, v, lax.rem(i + d, shares)), device_id_type=MESH,
        ).start()
    totals[i] = own[...]
    rest = totals.at[pl.ds(0, shares - 1)]
    pltpu.make_async_copy(rest, rest, t_recv).wait()
    mean_ref[...] = jnp.sum(totals[...], axis=0) / count
    pltpu.make_async_copy(seven, seven, s_send).wait()
    pltpu.make_async_copy(rest, rest, t_send).wait()


def losses_of(sums, shares):
    rows = sums.shape[1]
    vmem = pl.BlockSpec(memory_space=pltpu.VMEM)
    dma = pltpu.SemaphoreType.DMA
    return pl.pallas_call(
        functools.partial(losses_kernel, float(rows * shares)),
        out_shape=(jax.ShapeDtypeStruct((1, rows), jnp.float32), jax.ShapeDtypeStruct((8, 128), jnp.float32)),
        in_specs=[vmem],
        out_specs=(vmem, vmem),
        scratch_shapes=[
            pltpu.VMEM((8, 8, rows), jnp.float32),
            pltpu.VMEM((shares, 8, 128), jnp.float32),
            pltpu.VMEM((8, 128), jnp.float32),
            dma(()), dma(()), dma(()), dma(()),
        ],
        compiler_params=pltpu.CompilerParams(collective_id=1, has_side_effects=True),
        name="losses",
    )(sums)


def on_device(entering, depths, targets, norm_gain, w_gate, w_up, w_down, final_gain, head_weight):
    s, v = lax.axis_index("section"), lax.axis_index("vocab")
    micro, _, half, width = entering.shape
    active = jnp.broadcast_to((s < depths).astype(jnp.float32)[:, None, None], (micro, 1, width))
    finals = through_layers(
        entering[:, 0], active, norm_gain, final_gain[None, :], w_gate[0], w_up[0], w_down[0]
    )
    rows = micro * 2 * half
    columns = head_weight.shape[1]
    labels = targets.reshape(rows, 1) - (s * 2 + v) * columns
    labels = jnp.where(labels < columns, labels, -1)
    sums = head_sums(finals.reshape(rows, width), head_weight, jnp.broadcast_to(labels, (rows, 128)))
    loss, mean = losses_of(sums, lax.axis_size("dp"))
    return loss.reshape(targets.shape), mean[0, 0]


def solution(mesh):
    in_specs = (
        P(None, "dp", "vocab", None),
        P(),
        P(None, "dp", None),
        P("section", None),
        P("section", "dp", "vocab"),
        P("section", "dp", "vocab"),
        P("section", "vocab", "dp"),
        P(),
        P(None, ("section", "vocab")),
    )
    out_specs = (P(None, "dp", None), P())
    return jax.shard_map(
        on_device, mesh=mesh, in_specs=in_specs, out_specs=out_specs, check_vma=False
    )
```

time: 751 us -> 388 us (0.52); the launches traced: 764 us -> 386 us
  Pallas kernels: 0 us -> 340 us
  waiting for transfers between devices: 340 us -> 0 us
  matrix products: 156 us -> 0 us
  blocking collectives: 98.9 us -> 0 us
  starting transfers between devices: 76.9 us -> 0 us
  other arithmetic: 32.8 us -> 2.69 us
  loops' own time: 26.3 us -> 0 us
  local copies, waits for them, and re-layouts: 17.2 us -> 42.6 us
  between operations: 16.3 us -> 0.69 us
    pallas_call x0 -> x3, Pallas kernels: none -> 340 us  [the longest x1 308 us: through_layers(): pl.pallas_call(layers_kernel, out_shape=jax.ShapeDtypeStruct((2 * micro,...]
    all_gather x4 -> x0, waiting for transfers between devices: 326 us -> none  [the longest x1 110 us: on_device(): lax.all_gather(w_down, 'dp', axis=2, tiled=True)]
    dot_general x31 -> x0, matrix products: 156 us -> none  [the longest x10 78.8 us: apply_layer(): jnp.dot(block_rows, gate_full[layer_index], preferred_element_type=jnp.fl...]
    all_to_all x2 -> x0, blocking collectives: 41.9 us -> none  [copy_for_each(): return lax.all_to_all(copies, axis, split_axis=0, concat_axis=0, tiled=True)]
    unnamed x2 -> x5, local copies, waits for them, and re-layouts: 0.01 us -> 39.4 us
    ppermute x10 -> x0, starting transfers between devices: 38.9 us -> none  [passed_along(): return lax.ppermute(block, axis, route)]
    all_to_all x10 -> x0, starting transfers between devices: 37.9 us -> none  [summed_on_arrival(): parts = lax.all_to_all(cut_along(x, dim, size), axis, 0, 0, tiled=True)]
    all_gather x10 -> x0, blocking collectives: 29.7 us -> none  [apply_layer(): block_rows = lax.all_gather(normed, 'vocab', axis=0, tiled=True)]
  transfers between devices with their start and end apart: 24 -> 0, of which waited for: 14 -> 0; matrix products, arithmetic and copies ran while one was open for 1% -> 0% of each run, Pallas kernels for 0% -> 0%
where the time goes in v1:
time: 388 us; the launch traced here: 386 us
  Pallas kernels  340 us (88%)
  local copies, waits for them, and re-layouts  42.6 us (11%)
    pallas_call x1, Pallas kernels, through_layers(): pl.pallas_call(layers_kernel, out_shape=jax.ShapeDtypeStruct((2 * micro,...  308 us
    unnamed x5, local copies, waits for them, and re-layouts  39.4 us
    pallas_call x1, Pallas kernels, head_sums(): pl.pallas_call(functools.partial(head_kernel, columns), out_shape=jax.Sha...  16.8 us
    pallas_call x1, Pallas kernels, losses_of(): pl.pallas_call(functools.partial(losses_kernel, float(rows * shares)), ou...  15.7 us

profile of v1, /device:TPU:1, one launch (start us, length us, event | category | flops | bytes accessed | tf_op | source)
XLA Modules:
  0.0 386.4 jit_solution(5503147073381982565)
XLA Ops:
  0.6 0.7 subtract_reduce_fusion
  1.3 0.1 sub.16
  1.4 0.1 broadcast_in_dim.21.label_ref
  1.5 0.7 compare_convert_fusion
  2.2 0.7 broadcast_in_dim.18.act_ref
  2.9 307.9 %layers.1 = bf16[16,16,2048]{2,1,0:T(8,128)(2,1)} custom-call(bf16[8,16,2048]{2,1,0:T(8,128)(2,1)} %bitcast.12, f32[8,1,2048]{2,1,0:T(1,128)} %broadcast_in_dim.18.act_ref, f32[1,2048]{1,0:T(1,128)} %gain_ref.1, f32[1,2048]{1,0:T(1,128)} %bitcast.13, bf16[128,3584]{1,0:T(8,128)(2,1)} %bitcast.9, bf16[128,3584]{1,0:T(8,128)(2,1)} %bitcast.10, ...), custom_call_target="tpu_custom_call" | custom-call | tf_op jit(solution)/shard_map/layers/pallas_call | solution.py:222
  310.8 0.0 copy-start
  310.8 38.8 %copy.11.head_ref = bf16[2048,8016]{1,0:T(8,128)(2,1)} copy(bf16[2048,8016]{0,1:T(8,128)(2,1)} %param.17) | data formatting | bytes 65667072 | tf_op args[8]
  349.6 0.0 copy-done
  349.6 16.8 %head.1.sums_ref = f32[8,256]{1,0:T(8,128)S(1)} custom-call(bf16[256,2048]{1,0:T(8,128)(2,1)S(1)} %bitcast.8, bf16[2048,8016]{1,0:T(8,128)(2,1)} %copy.11.head_ref, s32[256,128]{1,0:T(8,128)S(1)} %broadcast_in_dim.21.label_ref), custom_call_target="tpu_custom_call" | custom-call | tf_op jit(solution)/shard_map/head/pallas_call | solution.py:288
  366.4 0.0 copy-start.1
  366.4 0.6 copy-done.1
  367.0 15.7 %losses.1 = (f32[1,256]{1,0:T(1,128)}, f32[8,128]{1,0:T(8,128)}) custom-call(f32[8,256]{1,0:T(8,128)} %copy-done.1), custom_call_target="tpu_custom_call" | custom-call | tf_op jit(solution)/shard_map/losses/pallas_call | solution.py:352
  382.8 0.5 broadcast.25
  383.3 1.3 reduce.7
  384.6 0.7 reshape.28
  385.3 1.2 slice.3
  (1 shorter events, 0.0 us)
Async XLA Ops:
  310.8 38.8 %copy-start = (bf16[16,16,2048]{2,1,0:T(8,128)(2,1)S(1)}, bf16[16,16,2048]{2,1,0:T(8,128)(2,1)}, u32[]{:S(2)}) copy-start(bf16[16,16,2048]{2,1,0:T(8,128)(2,1)} %layers.1) | copy-start | bytes 3145732
  366.4 0.6 copy-start.1

commit v2 on v1

--- a/solution.py
+++ b/solution.py
@@ -151,8 +151,10 @@
                     to(mine, mine, f_send.at[m], f_recv, (turned(s, d), w, i)).start()
             to(mine, mine, f_send.at[m], f_recv, (s, w_other, i)).start()
 
-    enter(0)
-    enter(1)
+    @pl.when(s == 0)
+    def _():
+        enter(0)
+        enter(1)
 
     for j in range(1, SIDE):
         await_block(j, 0)
@@ -166,6 +168,11 @@
     for j in range(SIDE):
         await_block(j, 2)
     pltpu.make_async_copy(three_bytes, three_bytes, own_sem).wait()
+
+    @pl.when(s > 0)
+    def _():
+        enter(0)
+        enter(1)
 
     def step(m, carry):
         branch(m)
@@ -246,8 +253,8 @@
 
 def head_kernel(columns, fin_ref, head_ref, label_ref, out_ref, peak, total, picked):
     j = pl.program_id(0)
-    rows, lanes = peak.shape
-    tile = head_ref.shape[1]
+    tile = head_ref.shape[0]
+    lines, rows = peak.shape
 
     @pl.when(j == 0)
     def _():
@@ -255,30 +262,25 @@
         total[...] = jnp.zeros_like(total)
         picked[...] = jnp.zeros_like(picked)
 
-    logits = jnp.dot(fin_ref[...], head_ref[...], preferred_element_type=jnp.float32)
-    at = j * tile + lax.broadcasted_iota(jnp.int32, (rows, lanes), 1)
-    groups = []
-    for g in range(tile // lanes):
-        groups.append(jnp.where(at + g * lanes < columns, logits[:, g * lanes : (g + 1) * lanes], -1e30))
+    logits = lax.dot_general(
+        head_ref[...], fin_ref[...], (((1,), (1,)), ((), ())), preferred_element_type=jnp.float32
+    )
+    at = lax.broadcasted_iota(jnp.int32, (tile, rows), 0)
+    logits = jnp.where(at < columns - j * tile, logits, -1e30)
+    found = jnp.where(at == label_ref[...] - j * tile, logits, 0.0)
+    values = logits.reshape(tile // lines, lines, rows)
     old = peak[...]
-    new = old
-    for values in groups:
-        new = jnp.maximum(new, values)
-    summed = total[...] * jnp.exp(old - new)
-    found = picked[...]
-    label = label_ref[...]
-    for g, values in enumerate(groups):
-        summed = summed + jnp.exp(values - new)
-        found = found + jnp.where(at + g * lanes == label, values, 0.0)
+    new = jnp.maximum(old, jnp.max(values, axis=0))
+    summed = total[...] * jnp.exp(old - new) + jnp.sum(jnp.exp(values - new), axis=0)
+    found = picked[...] + jnp.sum(found.reshape(values.shape), axis=0)
     peak[...], total[...], picked[...] = new, summed, found
 
     @pl.when(j == pl.num_programs(0) - 1)
     def _():
-        top = jnp.max(new, axis=1, keepdims=True)
-        whole = jnp.sum(summed * jnp.exp(new - top), axis=1, keepdims=True)
-        mine = jnp.sum(found, axis=1, keepdims=True)
-        for k, column in enumerate((top, whole, mine)):
-            out_ref[k : k + 1, :] = jnp.transpose(jnp.broadcast_to(column, (rows, lanes)))[0:1, :]
+        top = jnp.max(new, axis=0, keepdims=True)
+        out_ref[0:1, :] = top
+        out_ref[1:2, :] = jnp.sum(summed * jnp.exp(new - top), axis=0, keepdims=True)
+        out_ref[2:3, :] = jnp.sum(found, axis=0, keepdims=True)
         out_ref[3:8, :] = jnp.zeros((5, rows), jnp.float32)
 
 
@@ -291,14 +293,14 @@
         grid=(pl.cdiv(columns, tile),),
         in_specs=[
             pl.BlockSpec((rows, width), lambda j: (0, 0)),
-            pl.BlockSpec((width, tile), lambda j: (0, j)),
-            pl.BlockSpec((rows, 128), lambda j: (0, 0)),
+            pl.BlockSpec((tile, width), lambda j: (j, 0)),
+            pl.BlockSpec((1, rows), lambda j: (0, 0)),
         ],
         out_specs=pl.BlockSpec((8, rows), lambda j: (0, 0)),
-        scratch_shapes=[pltpu.VMEM((rows, 128), jnp.float32)] * 3,
+        scratch_shapes=[pltpu.VMEM((8, rows), jnp.float32)] * 3,
         compiler_params=pltpu.CompilerParams(vmem_limit_bytes=40 * 1024 * 1024),
         name="head",
-    )(finals, head_weight, labels)
+    )(finals, head_weight.T, labels)
 
 
 def losses_kernel(count, sums_ref, loss_ref, mean_ref, shared, totals, own, s_send, s_recv, t_send, t_recv):
@@ -374,9 +376,9 @@
     )
     rows = micro * 2 * half
     columns = head_weight.shape[1]
-    labels = targets.reshape(rows, 1) - (s * 2 + v) * columns
+    labels = targets.reshape(1, rows) - (s * 2 + v) * columns
     labels = jnp.where(labels < columns, labels, -1)
-    sums = head_sums(finals.reshape(rows, width), head_weight, jnp.broadcast_to(labels, (rows, 128)))
+    sums = head_sums(finals.reshape(rows, width), head_weight, labels)
     loss, mean = losses_of(sums, lax.axis_size("dp"))
     return loss.reshape(targets.shape), mean[0, 0]
 

time: 388 us -> 226 us (0.58)
  Pallas kernels: 340 us -> 218 us
  local copies, waits for them, and re-layouts: 42.6 us -> 4.97 us
    pallas_call x1, Pallas kernels: 308 us -> 187 us  [through_layers(): pl.pallas_call(layers_kernel, out_shape=jax.ShapeDtypeStruct((2 * micro,...]
    unnamed x5 -> x4, local copies, waits for them, and re-layouts: 39.4 us -> 1.81 us
where the time goes in v2:
time: 226 us
  Pallas kernels  218 us (96%)
  local copies, waits for them, and re-layouts  4.97 us (2%)
  other arithmetic  2.68 us (1%)
    pallas_call x1, Pallas kernels, through_layers(): pl.pallas_call(layers_kernel, out_shape=jax.ShapeDtypeStruct((2 * micro,...  187 us
    pallas_call x1, Pallas kernels, head_sums(): pl.pallas_call(functools.partial(head_kernel, columns), out_shape=jax.Sha...  16.6 us
    pallas_call x1, Pallas kernels, losses_of(): pl.pallas_call(functools.partial(losses_kernel, float(rows * shares)), ou...  14.5 us

profile of v2, /device:TPU:1, one launch (start us, length us, event | category | flops | bytes accessed | tf_op | source)
XLA Modules:
  0.0 226.0 jit_solution(7650768981861823790)
XLA Ops:
  0.6 0.7 subtract_reduce_fusion
  1.3 0.1 sub.19
  1.4 0.7 compare_convert_fusion
  2.1 0.7 broadcast_in_dim.13.act_ref
  2.8 186.6 %layers.1 = bf16[16,16,2048]{2,1,0:T(8,128)(2,1)} custom-call(bf16[8,16,2048]{2,1,0:T(8,128)(2,1)} %bitcast.14, f32[8,1,2048]{2,1,0:T(1,128)} %broadcast_in_dim.13.act_ref, f32[1,2048]{1,0:T(1,128)} %gain_ref.1, f32[1,2048]{1,0:T(1,128)} %bitcast.15, bf16[128,3584]{1,0:T(8,128)(2,1)} %bitcast.11, bf16[128,3584]{1,0:T(8,128)(2,1)} %bitcast.12, ...), custom_call_target="tpu_custom_call" | custom-call | tf_op jit(solution)/shard_map/layers/pallas_call | solution.py:229
  189.4 0.0 copy-start
  189.4 1.2 copy-done
  190.6 16.6 %head.1.sums_ref = f32[8,256]{1,0:T(8,128)S(1)} custom-call(bf16[256,2048]{1,0:T(8,128)(2,1)S(1)} %bitcast.9, bf16[8016,2048]{1,0:T(8,128)(2,1)} %bitcast.10, s32[1,256]{1,0:T(1,128)S(1)} %compare_select_fusion.label_ref), custom_call_target="tpu_custom_call" | custom-call | tf_op jit(solution)/shard_map/head/pallas_call | solution.py:290
  207.2 0.0 copy-start.1
  207.2 0.6 copy-done.1
  207.8 14.5 %losses.1 = (f32[1,256]{1,0:T(1,128)}, f32[8,128]{1,0:T(8,128)}) custom-call(f32[8,256]{1,0:T(8,128)} %copy-done.1), custom_call_target="tpu_custom_call" | custom-call | tf_op jit(solution)/shard_map/losses/pallas_call | solution.py:354
  222.3 0.5 broadcast.34
  222.8 1.3 reduce.7
  224.1 0.7 reshape.37
  224.8 1.2 slice.3
  (1 shorter events, 0.0 us)
Async XLA Ops:
  189.4 1.2 copy-start
  207.2 0.6 copy-start.1

commit v3 on v2

v3 whole, which is shorter than its diff:
```python
import jax
import jax.numpy as jnp
from jax import lax
from jax.experimental import pallas as pl
from jax.experimental.pallas import tpu as pltpu
from jax.sharding import PartitionSpec as P

EPS = 1e-05
MESH = pl.DeviceIdType.MESH
SIDE = 4


def rms_scaled(values, gain):
    widened = values.astype(jnp.float32)
    return widened * lax.rsqrt(jnp.mean(widened * widened, axis=-1, keepdims=True) + EPS) * gain


def place():
    s, v, i = lax.axis_index("section"), lax.axis_index("vocab"), lax.axis_index("dp")
    z, y = lax.div(i, SIDE), lax.rem(i, SIDE)
    return s, v, i, y + v * (z - y), z + v * (y - z)


def dp_of(v, a, b):
    return SIDE * b + a + v * (SIDE - 1) * (a - b)


def turned(x, d):
    return lax.rem(x + d, SIDE)


def window_kernel(
    depth_ref, ent_ref, gain_ref, fgain_ref, label_ref, wg_ref, wu_ref, wd_ref, head_ref,
    loss_ref, mean_ref,
    wgu, wdn, gat, part, arr, xin, xout, hid, fin, fin_t, head, peak, total, picked, shared, totals,
    own_sem, w_send, w_recv, ag_send, ag_recv, rs_send, rs_recv, x_send, x_recv, f_send, f_recv,
    h_sem, s_send, s_recv, t_send, t_recv,
):
    s, v, i, a, b = place()
    micro, half, width = ent_ref.shape
    hb = hid.shape[1]
    fr = wg_ref.shape[0]
    columns = head_ref.shape[0]
    shares = totals.shape[0]
    w_other = 1 - v
    last = SIDE - 1
    heads = 2 * SIDE

    def to(src, dst, send, recv, where):
        return pltpu.make_async_remote_copy(
            src_ref=src, dst_ref=dst, send_sem=send, recv_sem=recv, device_id=where, device_id_type=MESH
        )

    def await_bytes(ref, sem):
        pltpu.make_async_copy(ref, ref, sem).wait()

    barrier = pltpu.get_barrier_semaphore()

    def greet(where):
        pl.semaphore_signal(barrier, inc=1, device_id=where, device_id_type=MESH)

    for d in range(1, SIDE):
        for w in (0, 1):
            greet((s, w, dp_of(v, turned(a, d), b)))
            greet((s, w, dp_of(v, a, turned(b, d))))
            greet((turned(s, d), w, i))
        for e in range(1, SIDE):
            greet((s, v, dp_of(v, turned(a, d), turned(b, e))))
    greet((s, w_other, i))
    pl.semaphore_wait(barrier, last * (6 + last) + 1)

    def landing(k):
        rows = pl.ds(pl.multiple_of(k * fr, fr), fr)
        return wgu.at[rows, pl.ds(0, hb)], wgu.at[rows, pl.ds(hb, hb)], wdn.at[:, rows]

    def held(k):
        units = pl.ds(pl.multiple_of(k * hb, hb), hb)
        return wg_ref.at[:, units], wu_ref.at[:, units], wd_ref.at[units, :]

    def three(sources, k, send, recv, where):
        for src, dst in zip(sources, landing(k)):
            to(src, dst, send, recv, where).start()

    three_bytes = wgu.at[pl.ds(0, 3 * fr), pl.ds(0, hb)]

    def await_block(j, d):
        await_bytes(three_bytes, w_recv.at[turned(a, j) * SIDE + turned(b, d)])

    right = (s, v, dp_of(v, a, turned(b, 1)))
    left = (s, v, dp_of(v, a, turned(b, last)))

    def pass_round(j, sources):
        k = dp_of(v, turned(a, j), b)
        recv = w_recv.at[turned(a, j) * SIDE + b]
        three(sources, k, w_send.at[3 + 2 * j], recv, right)
        three(sources, k, w_send.at[4 + 2 * j], recv, left)

    for src, dst in zip(held(a), landing(i)):
        pltpu.make_async_copy(src, dst, own_sem).start()
    for d in range(1, SIDE):
        peer = turned(a, d)
        three(held(peer), i, w_send.at[d - 1], w_recv.at[a * SIDE + b], (s, v, dp_of(v, peer, b)))
    pass_round(0, held(a))

    def to_group(src, block_own, block_other, send, recv):
        for d in range(1, SIDE):
            to(src, gat.at[block_own], send, recv, (s, v, dp_of(v, turned(a, d), b))).start()
        for d in range(SIDE):
            to(src, gat.at[block_other], send, recv, (s, w_other, dp_of(v, a, turned(b, d)))).start()

    def enter(m):
        @pl.when(s == 0)
        def _():
            xin[m] = ent_ref[m]

        @pl.when(s > 0)
        def _():
            await_bytes(xin.at[m], x_recv.at[m])

        mine = m * 8 + a * 2 + v
        gat[mine] = rms_scaled(xin[m], gain_ref[...]).astype(jnp.bfloat16)
        to_group(gat.at[mine], mine, m * 8 + b * 2 + v, ag_send.at[m], ag_recv.at[m])

    def branch(m):
        seven = gat.at[pl.ds(0, 7)]
        await_bytes(seven, ag_recv.at[m])
        rows = gat[pl.ds(pl.multiple_of(m * 8, 8), 8)].reshape(8 * half, width)
        both = jnp.dot(rows, wgu[...], preferred_element_type=jnp.float32)
        gate, up = both[:, :hb], both[:, hb:]
        hid[...] = (gate / (1.0 + jnp.exp(-gate)) * up).astype(jnp.bfloat16)
        out = jnp.dot(hid[...], wdn[...], preferred_element_type=jnp.float32)
        part[pl.ds(pl.multiple_of(m * 8, 8), 8)] = out.astype(jnp.bfloat16).reshape(8, half, width)
        slot = m * 8 + v * SIDE + a
        for d in range(1, SIDE):
            c = turned(a, d)
            for w in (0, 1):
                to(part.at[m * 8 + c * 2 + w], arr.at[slot], rs_send.at[m], rs_recv.at[m],
                   (s, w, dp_of(v, c, b))).start()
        to(part.at[m * 8 + a * 2 + w_other], arr.at[slot], rs_send.at[m], rs_recv.at[m], (s, w_other, i)).start()
        arr[slot] = part[m * 8 + a * 2 + v]

    def leave(m):
        seven = arr.at[pl.ds(0, 7)]
        await_bytes(seven, rs_recv.at[m])
        added = arr[m * 8].astype(jnp.float32)
        for k in range(1, 8):
            added = added + arr[m * 8 + k].astype(jnp.float32)
        state = xin[m].astype(jnp.float32)
        active = jnp.full(state.shape, depth_ref[m], jnp.int32) > s
        state = jnp.where(active, state + added, state).astype(jnp.bfloat16)

        @pl.when(s < last)
        def _():
            xout[m] = state
            to(xout.at[m], xin.at[m], x_send.at[m], x_recv.at[m], (s + 1, v, i)).start()

        @pl.when(s == last)
        def _():
            fin[m * 2 + v] = rms_scaled(state, fgain_ref[...]).astype(jnp.bfloat16)
            mine = fin.at[m * 2 + v]
            for d in range(1, SIDE):
                for w in (0, 1):
                    to(mine, mine, f_send.at[m], f_recv, (turned(s, d), w, i)).start()
            to(mine, mine, f_send.at[m], f_recv, (s, w_other, i)).start()

    @pl.when(s == 0)
    def _():
        enter(0)
        enter(1)

    pltpu.make_async_copy(head_ref, head, h_sem).start()

    for j in range(1, SIDE):
        await_block(j, 0)
        pass_round(j, landing(dp_of(v, turned(a, j), b)))
    for j in range(SIDE):
        d, where = (last, right) if j % 2 == 0 else (1, left)
        await_block(j, d)
        k = dp_of(v, turned(a, j), turned(b, d))
        three(landing(k), k, w_send.at[11 + j], w_recv.at[turned(a, j) * SIDE + turned(b, d)], where)
        await_block(j, SIDE - d)
    for j in range(SIDE):
        await_block(j, 2)
    await_bytes(three_bytes, own_sem)

    @pl.when(s > 0)
    def _():
        enter(0)
        enter(1)

    def step(m, carry):
        branch(m)

        @pl.when(m > 0)
        def _():
            leave(m - 1)

        @pl.when(m + 2 < micro)
        def _():
            enter(m + 2)

        return carry

    lax.fori_loop(0, micro, step, 0)
    leave(micro - 1)

    await_bytes(head, h_sem)

    @pl.when(s < last)
    def _():
        await_bytes(fin, f_recv)

    @pl.when(s == last)
    def _():
        await_bytes(fin.at[pl.ds(0, micro)], f_recv)

    lines, positions = peak.shape
    fin_t[...] = jnp.transpose(fin[...].reshape(positions, width))
    peak[...] = jnp.full_like(peak, -1e30)
    total[...] = jnp.zeros_like(total)
    picked[...] = jnp.zeros_like(picked)
    labels = label_ref[...]

    def tile_sums(start, size):
        logits = jnp.dot(head[pl.ds(start, size), :], fin_t[...], preferred_element_type=jnp.float32)
        at = lax.broadcasted_iota(jnp.int32, (size, positions), 0)
        found = jnp.where(at == labels - start, logits, 0.0)
        values = logits.reshape(size // lines, lines, positions)
        old = peak[...]
        new = jnp.maximum(old, jnp.max(values, axis=0))
        total[...] = total[...] * jnp.exp(old - new) + jnp.sum(jnp.exp(values - new), axis=0)
        picked[...] = picked[...] + jnp.sum(found.reshape(values.shape), axis=0)
        peak[...] = new

    tile = TILE
    full = columns // tile

    def one_tile(j, carry):
        tile_sums(pl.multiple_of(j * tile, tile), tile)
        return carry

    lax.fori_loop(0, full, one_tile, 0)
    if columns % tile:
        tile_sums(full * tile, columns % tile)

    me = s * 2 + v
    new = peak[...]
    top = jnp.max(new, axis=0, keepdims=True)
    shared[me, 0:1, :] = top
    shared[me, 1:2, :] = jnp.sum(total[...] * jnp.exp(new - top), axis=0, keepdims=True)
    shared[me, 2:3, :] = jnp.sum(picked[...], axis=0, keepdims=True)
    shared[me, 3:8, :] = jnp.zeros((5, positions), jnp.float32)
    mine = shared.at[me]
    for d in range(SIDE):
        for w in (0, 1):
            if d:
                to(mine, mine, s_send, s_recv, (turned(s, d), w, i)).start()
    to(mine, mine, s_send, s_recv, (s, w_other, i)).start()
    seven = shared.at[pl.ds(0, heads - 1)]
    await_bytes(seven, s_recv)
    everyone = shared[...]
    peaks = everyone[:, 0, :]
    top = jnp.max(peaks, axis=0, keepdims=True)
    summed = jnp.sum(everyone[:, 1, :] * jnp.exp(peaks - top), axis=0, keepdims=True)
    loss = jnp.log(summed) + top - jnp.sum(everyone[:, 2, :], axis=0, keepdims=True)
    totals[i] = jnp.broadcast_to(jnp.sum(loss, axis=1, keepdims=True), totals.shape[1:])
    for d in range(1, shares):
        to(totals.at[i], totals.at[i], t_send, t_recv, (s, v, lax.rem(i + d, shares))).start()
    for m in range(micro):
        loss_ref[m] = loss[:, 2 * half * m : 2 * half * (m + 1)]

    for k in range(15):
        await_bytes(three_bytes, w_send.at[k])

    def drain(m, carry):
        await_bytes(gat.at[pl.ds(0, heads - 1)], ag_send.at[m])
        await_bytes(gat.at[pl.ds(0, heads - 1)], rs_send.at[m])

        @pl.when(s < last)
        def _():
            await_bytes(xout.at[0], x_send.at[m])

        @pl.when(s == last)
        def _():
            await_bytes(gat.at[pl.ds(0, heads - 1)], f_send.at[m])

        return carry

    lax.fori_loop(0, micro, drain, 0)
    await_bytes(seven, s_send)
    rest = totals.at[pl.ds(0, shares - 1)]
    await_bytes(rest, t_recv)
    mean_ref[...] = jnp.sum(totals[...], axis=0)[0:1, 0:1] / float(shares * positions)
    await_bytes(rest, t_send)


TILE = 1024


def on_device(entering, depths, targets, norm_gain, w_gate, w_up, w_down, final_gain, head_weight):
    s, v, shares = lax.axis_index("section"), lax.axis_index("vocab"), lax.axis_size("dp")
    micro, _, half, width = entering.shape
    columns = head_weight.shape[1]
    hb = w_gate.shape[2] // SIDE
    positions = micro * 2 * half
    labels = targets.reshape(1, positions) - (s * 2 + v) * columns
    vmem, any_space = pl.BlockSpec(memory_space=pltpu.VMEM), pl.BlockSpec(memory_space=pl.ANY)
    dma, held = pltpu.SemaphoreType.DMA, pltpu.VMEM
    bf16, f32 = jnp.bfloat16, jnp.float32
    rows = (half, width)
    return pl.pallas_call(
        window_kernel,
        out_shape=(
            jax.ShapeDtypeStruct((micro, 1, 2 * half), f32),
            jax.ShapeDtypeStruct((1, 1), f32),
        ),
        in_specs=[pl.BlockSpec(memory_space=pltpu.SMEM)] + [vmem] * 4 + [any_space] * 4,
        out_specs=(vmem, vmem),
        scratch_shapes=[
            held((width, 2 * hb), bf16),
            held((hb, width), bf16),
            held((micro * 2 * SIDE, *rows), bf16),
            held((micro * 2 * SIDE, *rows), bf16),
            held((micro * 2 * SIDE, *rows), bf16),
            held((micro, *rows), bf16),
            held((micro, *rows), bf16),
            held((2 * SIDE * half, hb), bf16),
            held((micro * 2, *rows), bf16),
            held((width, positions), bf16),
            held((columns, width), bf16),
            held((8, positions), f32), held((8, positions), f32), held((8, positions), f32),
            held((2 * SIDE, 8, positions), f32),
            held((shares, 8, 128), f32),
            dma(()), dma((15,)), dma((SIDE * SIDE,)),
            dma((micro,)), dma((micro,)), dma((micro,)), dma((micro,)),
            dma((micro,)), dma((micro,)), dma((micro,)), dma(()),
            dma(()), dma(()), dma(()), dma(()), dma(()),
        ],
        compiler_params=pltpu.CompilerParams(
            collective_id=0, has_side_effects=True, vmem_limit_bytes=67043328
        ),
        name="window",
    )(depths, entering[:, 0], norm_gain, final_gain[None, :], labels, w_gate[0], w_up[0], w_down[0], head_weight.T)


def per_device(*args):
    loss, mean = on_device(*args)
    return loss, mean.reshape(())


def solution(mesh):
    in_specs = (
        P(None, "dp", "vocab", None),
        P(),
        P(None, "dp", None),
        P("section", None),
        P("section", "dp", "vocab"),
        P("section", "dp", "vocab"),
        P("section", "vocab", "dp"),
        P(),
        P(None, ("section", "vocab")),
    )
    out_specs = (P(None, "dp", None), P())
    return jax.shard_map(
        per_device, mesh=mesh, in_specs=in_specs, out_specs=out_specs, check_vma=False
    )
```

time: 226 us -> 213 us (0.942)
  Pallas kernels: 218 us -> 208 us
  local copies, waits for them, and re-layouts: 4.97 us -> 1.92 us
    pallas_call x3 -> x1, Pallas kernels: 218 us -> 208 us  [on_device(): pl.pallas_call(window_kernel, out_shape=(jax.ShapeDtypeStruct((micro, 1,...]
where the time goes in v3:
time: 213 us
  Pallas kernels  208 us (98%)
  between operations  2.34 us (1%)
    pallas_call x1, Pallas kernels, on_device(): pl.pallas_call(window_kernel, out_shape=(jax.ShapeDtypeStruct((micro, 1,...  208 us

profile of v3, /device:TPU:1, one launch (start us, length us, event | category | flops | bytes accessed | tf_op | source)
XLA Modules:
  0.0 213.0 jit_solution(5313094539211169607)
XLA Ops:
  0.6 0.7 subtract_reduce_fusion
  1.3 0.6 sub.10.label_ref
  2.0 208.1 %window.1 = (f32[8,1,32]{2,1,0:T(1,128)}, f32[1,1]{1,0:T(1,128)}) custom-call(s32[8]{0:T(128)} %depth_ref.1, bf16[8,16,2048]{2,1,0:T(8,128)(2,1)} %bitcast.11, f32[1,2048]{1,0:T(1,128)} %gain_ref.1, f32[1,2048]{1,0:T(1,128)} %bitcast.12, s32[1,256]{1,0:T(1,128)} %sub.10.label_ref, bf16[128,3584]{1,0:T(8,128)(2,1)} %bitcast.8, bf16[128,3584]{1,0:T(8,128)(2,1)} %bitcast.9, ...), custom_call_target="tpu_custom_call" | custom-call | tf_op jit(solution)/shard_map/window/pallas_call | solution.py:311
  210.1 1.3 copy.13

commit v4 on v3

--- a/solution.py
+++ b/solution.py
@@ -10,6 +10,9 @@
 SIDE = 4
 
 
+DETOURS = ((0, 3, 0), (1, 1, 1))
+
+
 def rms_scaled(values, gain):
     widened = values.astype(jnp.float32)
     return widened * lax.rsqrt(jnp.mean(widened * widened, axis=-1, keepdims=True) + EPS) * gain
@@ -34,7 +37,7 @@
     loss_ref, mean_ref,
     wgu, wdn, gat, part, arr, xin, xout, hid, fin, fin_t, head, peak, total, picked, shared, totals,
     own_sem, w_send, w_recv, ag_send, ag_recv, rs_send, rs_recv, x_send, x_recv, f_send, f_recv,
-    h_sem, s_send, s_recv, t_send, t_recv,
+    st_send, st_recv, h_sem, s_send, s_recv, t_send, t_recv,
 ):
     s, v, i, a, b = place()
     micro, half, width = ent_ref.shape
@@ -66,8 +69,10 @@
             greet((turned(s, d), w, i))
         for e in range(1, SIDE):
             greet((s, v, dp_of(v, turned(a, d), turned(b, e))))
+    for d in (1, last):
+        greet((turned(s, d), v, dp_of(v, a, turned(b, 2))))
     greet((s, w_other, i))
-    pl.semaphore_wait(barrier, last * (6 + last) + 1)
+    pl.semaphore_wait(barrier, last * (6 + last) + 3)
 
     def landing(k):
         rows = pl.ds(pl.multiple_of(k * fr, fr), fr)
@@ -101,6 +106,35 @@
         peer = turned(a, d)
         three(held(peer), i, w_send.at[d - 1], w_recv.at[a * SIDE + b], (s, v, dp_of(v, peer, b)))
     pass_round(0, held(a))
+
+    def stage(n):
+        top = n * (fr + hb)
+        return (
+            head.at[pl.ds(top, fr), pl.ds(0, hb)],
+            head.at[pl.ds(top, fr), pl.ds(hb, hb)],
+            head.at[pl.ds(top + fr, hb), pl.ds(0, fr)],
+        )
+
+    def detour(j, sources):
+        for n, (turn, helper, _) in enumerate(DETOURS):
+            if turn == j:
+                @pl.when(s == 0)
+                def _():
+                    where = (helper, v, dp_of(v, a, turned(b, 2)))
+                    for src, dst in zip(sources, stage(n)):
+                        to(src, dst, w_send.at[11 + j], st_recv.at[n], where).start()
+
+    def help_on(j):
+        for n, (turn, helper, after) in enumerate(DETOURS):
+            if after == j:
+                @pl.when(s == helper)
+                def _():
+                    await_bytes(three_bytes, st_recv.at[n])
+                    k = dp_of(v, turned(a, turn), turned(b, 2))
+                    recv = w_recv.at[turned(a, turn) * SIDE + turned(b, 2)]
+                    three(stage(n), k, st_send.at[n], recv, (0, v, i))
+
+    detour(0, held(a))
 
     def to_group(src, block_own, block_other, send, recv):
         for d in range(1, SIDE):
@@ -168,20 +202,36 @@
         enter(0)
         enter(1)
 
-    pltpu.make_async_copy(head_ref, head, h_sem).start()
-
     for j in range(1, SIDE):
         await_block(j, 0)
-        pass_round(j, landing(dp_of(v, turned(a, j), b)))
+        block = landing(dp_of(v, turned(a, j), b))
+        pass_round(j, block)
+        detour(j, block)
+    help_on(-1)
     for j in range(SIDE):
         d, where = (last, right) if j % 2 == 0 else (1, left)
         await_block(j, d)
         k = dp_of(v, turned(a, j), turned(b, d))
-        three(landing(k), k, w_send.at[11 + j], w_recv.at[turned(a, j) * SIDE + turned(b, d)], where)
+
+        def forward():
+            three(landing(k), k, w_send.at[11 + j], w_recv.at[turned(a, j) * SIDE + turned(b, d)], where)
+
+        if any(turn == j for turn, _, _ in DETOURS):
+            pl.when(s != 0)(forward)
+        else:
+            forward()
         await_block(j, SIDE - d)
+        help_on(j)
     for j in range(SIDE):
         await_block(j, 2)
     await_bytes(three_bytes, own_sem)
+
+    for n, (_, helper, _) in enumerate(DETOURS):
+        @pl.when(s == helper)
+        def _():
+            await_bytes(three_bytes, st_send.at[n])
+
+    pltpu.make_async_copy(head_ref, head, h_sem).start()
 
     @pl.when(s > 0)
     def _():
@@ -235,11 +285,12 @@
     tile = TILE
     full = columns // tile
 
-    def one_tile(j, carry):
-        tile_sums(pl.multiple_of(j * tile, tile), tile)
+    def some_tiles(j, carry):
+        for k in range(3):
+            tile_sums(pl.multiple_of((j * 3 + k) * tile, tile), tile)
         return carry
 
-    lax.fori_loop(0, full, one_tile, 0)
+    lax.fori_loop(0, full // 3, some_tiles, 0)
     if columns % tile:
         tile_sums(full * tile, columns % tile)
 
@@ -294,7 +345,7 @@
     await_bytes(rest, t_send)
 
 
-TILE = 1024
+TILE = 512
 
 
 def on_device(entering, depths, targets, norm_gain, w_gate, w_up, w_down, final_gain, head_weight):
@@ -334,7 +385,7 @@
             dma(()), dma((15,)), dma((SIDE * SIDE,)),
             dma((micro,)), dma((micro,)), dma((micro,)), dma((micro,)),
             dma((micro,)), dma((micro,)), dma((micro,)), dma(()),
-            dma(()), dma(()), dma(()), dma(()), dma(()),
+            dma((len(DETOURS),)), dma((len(DETOURS),)), dma(()), dma(()), dma(()), dma(()), dma(()),
         ],
         compiler_params=pltpu.CompilerParams(
             collective_id=0, has_side_effects=True, vmem_limit_bytes=67043328

time: 213 us -> 208 us (0.977)
  Pallas kernels: 208 us -> 203 us
    pallas_call x1, Pallas kernels: 208 us -> 203 us  [on_device(): pl.pallas_call(window_kernel, out_shape=(jax.ShapeDtypeStruct((micro, 1,...]
where the time goes in v4:
time: 208 us
  Pallas kernels  203 us (98%)
  between operations  2.34 us (1%)
    pallas_call x1, Pallas kernels, on_device(): pl.pallas_call(window_kernel, out_shape=(jax.ShapeDtypeStruct((micro, 1,...  203 us

profile of v4, /device:TPU:1, one launch (start us, length us, event | category | flops | bytes accessed | tf_op | source)
XLA Modules:
  0.0 208.0 jit_solution(4564229059833735946)
XLA Ops:
  0.6 0.7 subtract_reduce_fusion
  1.3 0.6 sub.10.label_ref
  2.0 203.0 %window.1 = (f32[8,1,32]{2,1,0:T(1,128)}, f32[1,1]{1,0:T(1,128)}) custom-call(s32[8]{0:T(128)} %depth_ref.1, bf16[8,16,2048]{2,1,0:T(8,128)(2,1)} %bitcast.11, f32[1,2048]{1,0:T(1,128)} %gain_ref.1, f32[1,2048]{1,0:T(1,128)} %bitcast.12, s32[1,256]{1,0:T(1,128)} %sub.10.label_ref, bf16[128,3584]{1,0:T(8,128)(2,1)} %bitcast.8, bf16[128,3584]{1,0:T(8,128)(2,1)} %bitcast.9, ...), custom_call_target="tpu_custom_call" | custom-call | tf_op jit(solution)/shard_map/window/pallas_call | solution.py:362
  205.0 1.3 copy.13

commit v5 on v4

--- a/solution.py
+++ b/solution.py
@@ -35,9 +35,9 @@
 def window_kernel(
     depth_ref, ent_ref, gain_ref, fgain_ref, label_ref, wg_ref, wu_ref, wd_ref, head_ref,
     loss_ref, mean_ref,
-    wgu, wdn, gat, part, arr, xin, xout, hid, fin, fin_t, head, peak, total, picked, shared, totals,
+    wgu, wdn, gat, part, arr, xin, xout, hid, fin, fin_t, head, label, peak, total, picked, shared, totals,
     own_sem, w_send, w_recv, ag_send, ag_recv, rs_send, rs_recv, x_send, x_recv, f_send, f_recv,
-    st_send, st_recv, h_sem, s_send, s_recv, t_send, t_recv,
+    st_send, st_recv, e_sem, h_sem, s_send, s_recv, t_send, t_recv,
 ):
     s, v, i, a, b = place()
     micro, half, width = ent_ref.shape
@@ -56,6 +56,10 @@
 
     def await_bytes(ref, sem):
         pltpu.make_async_copy(ref, ref, sem).wait()
+
+    @pl.when(s == 0)
+    def _():
+        pltpu.make_async_copy(ent_ref, xin, e_sem).start()
 
     barrier = pltpu.get_barrier_semaphore()
 
@@ -143,10 +147,6 @@
             to(src, gat.at[block_other], send, recv, (s, w_other, dp_of(v, a, turned(b, d)))).start()
 
     def enter(m):
-        @pl.when(s == 0)
-        def _():
-            xin[m] = ent_ref[m]
-
         @pl.when(s > 0)
         def _():
             await_bytes(xin.at[m], x_recv.at[m])
@@ -199,6 +199,7 @@
 
     @pl.when(s == 0)
     def _():
+        await_bytes(xin, e_sem)
         enter(0)
         enter(1)
 
@@ -269,7 +270,9 @@
     peak[...] = jnp.full_like(peak, -1e30)
     total[...] = jnp.zeros_like(total)
     picked[...] = jnp.zeros_like(picked)
-    labels = label_ref[...]
+    for m in range(micro):
+        label[:, 2 * half * m : 2 * half * (m + 1)] = label_ref[m]
+    labels = label[...] - (s * 2 + v) * columns
 
     def tile_sums(start, size):
         logits = jnp.dot(head[pl.ds(start, size), :], fin_t[...], preferred_element_type=jnp.float32)
@@ -349,12 +352,11 @@
 
 
 def on_device(entering, depths, targets, norm_gain, w_gate, w_up, w_down, final_gain, head_weight):
-    s, v, shares = lax.axis_index("section"), lax.axis_index("vocab"), lax.axis_size("dp")
+    shares = lax.axis_size("dp")
     micro, _, half, width = entering.shape
     columns = head_weight.shape[1]
     hb = w_gate.shape[2] // SIDE
     positions = micro * 2 * half
-    labels = targets.reshape(1, positions) - (s * 2 + v) * columns
     vmem, any_space = pl.BlockSpec(memory_space=pltpu.VMEM), pl.BlockSpec(memory_space=pl.ANY)
     dma, held = pltpu.SemaphoreType.DMA, pltpu.VMEM
     bf16, f32 = jnp.bfloat16, jnp.float32
@@ -365,7 +367,7 @@
             jax.ShapeDtypeStruct((micro, 1, 2 * half), f32),
             jax.ShapeDtypeStruct((1, 1), f32),
         ),
-        in_specs=[pl.BlockSpec(memory_space=pltpu.SMEM)] + [vmem] * 4 + [any_space] * 4,
+        in_specs=[pl.BlockSpec(memory_space=pltpu.SMEM), any_space] + [vmem] * 3 + [any_space] * 4,
         out_specs=(vmem, vmem),
         scratch_shapes=[
             held((width, 2 * hb), bf16),
@@ -379,19 +381,20 @@
             held((micro * 2, *rows), bf16),
             held((width, positions), bf16),
             held((columns, width), bf16),
+            held((1, positions), jnp.int32),
             held((8, positions), f32), held((8, positions), f32), held((8, positions), f32),
             held((2 * SIDE, 8, positions), f32),
             held((shares, 8, 128), f32),
             dma(()), dma((15,)), dma((SIDE * SIDE,)),
             dma((micro,)), dma((micro,)), dma((micro,)), dma((micro,)),
             dma((micro,)), dma((micro,)), dma((micro,)), dma(()),
-            dma((len(DETOURS),)), dma((len(DETOURS),)), dma(()), dma(()), dma(()), dma(()), dma(()),
+            dma((len(DETOURS),)), dma((len(DETOURS),)), dma(()), dma(()), dma(()), dma(()), dma(()), dma(()),
         ],
         compiler_params=pltpu.CompilerParams(
             collective_id=0, has_side_effects=True, vmem_limit_bytes=67043328
         ),
         name="window",
-    )(depths, entering[:, 0], norm_gain, final_gain[None, :], labels, w_gate[0], w_up[0], w_down[0], head_weight.T)
+    )(depths, entering[:, 0], norm_gain, final_gain[None, :], targets, w_gate[0], w_up[0], w_down[0], head_weight.T)
 
 
 def per_device(*args):

time: 208 us -> 207 us (level)
  no operation moved by 1% of the time
where the time goes in v5:
time: 207 us; the launch traced here: 206 us
  Pallas kernels  203 us (98%)
  between operations  2.41 us (1%)
    pallas_call x1, Pallas kernels, on_device(): pl.pallas_call(window_kernel, out_shape=(jax.ShapeDtypeStruct((micro, 1,...  203 us

profile of v5, /device:TPU:1, one launch (start us, length us, event | category | flops | bytes accessed | tf_op | source)
XLA Modules:
  0.0 206.4 jit_solution(14981474549938822598)
XLA Ops:
  0.6 202.8 %window.1 = (f32[8,1,32]{2,1,0:T(1,128)}, f32[1,1]{1,0:T(1,128)}) custom-call(s32[8]{0:T(128)} %depth_ref.1, bf16[8,16,2048]{2,1,0:T(8,128)(2,1)} %bitcast.11, f32[1,2048]{1,0:T(1,128)} %gain_ref.1, f32[1,2048]{1,0:T(1,128)} %bitcast.12, s32[8,1,32]{2,1,0:T(1,128)} %label_ref.1, bf16[128,3584]{1,0:T(8,128)(2,1)} %bitcast.8, bf16[128,3584]{1,0:T(8,128)(2,1)} %bitcast.9, ...), custom_call_target="tpu_custom_call" | custom-call | tf_op jit(solution)/shard_map/window/pallas_call | solution.py:364
  203.4 1.3 copy.13
